TPU v7x, 256 devices: a whole 4x4x8 slice. The times are simulated.
256 devices in a mesh: src: 4 (over x), space: 64 (over z, y, core).
Axes of the slice: x: 4, y: 4, z: 8, core: 2. Of those that a mesh axis runs over, the one named last changes fastest.
Arguments:
- contrast: float32 [2, 64, 256, 256], P(None, None, 'space'), may hold values from -0.4 to 0.45
- measured: float32 [4, 2, 256, 256], P('src', None, 'space'), may hold values from -7 to 7
- positions: int32 [4, 2], P('src'), may hold values from 0 to 255
Outputs:
- contrast_sources: float32 [4, 2, 64, 256, 256], P('src', None, None, 'space')
- contrast_new: float32 [2, 64, 256, 256], P(None, None, 'space')
All inputs are finite; a program needn't handle non-finite values.
Results may differ from a plain program's by a relative error of at most 0.0003.
Values sent between devices are 32-bit elements; how exact they have to be, the bound alone decides.
A program may use at most 64 MiB of HBM per device.

v0:
```python
from functools import partial
import math
import jax
import jax.numpy as jnp
from jax import lax
from jax.sharding import PartitionSpec as P

NX = 256
NY = 256
NZ = 64
OUTER = 2
WAVENUMBER = 2.0 * math.pi / 6.0
DAMPING = 0.3
SOURCE_GAP = 8.0
FLOOR_SHARE = 0.75
REAL_LOW = -0.25
REAL_HIGH = 0.35
IMAG_HIGH = 0.1
DEPTH_PATTERN = "akbn,sbnxy->sakxy"
FIRST_PATTERN = "akbn,sbznj->sazkj"
SECOND_PATTERN = "akbn,sbzxn->sazxk"


def laplace_modes(start_mode, length, total):
    mode_index = (start_mode + jnp.arange(length)).astype(jnp.float32)
    half_sine = jnp.sin(math.pi * mode_index / total)
    return 4.0 * half_sine * half_sine


def green_spectrum(depth_modes, first_modes, second_modes):
    eigen = depth_modes[:, None, None] + first_modes[None, :, None] + second_modes[None, None, :]
    wave_sq = WAVENUMBER * WAVENUMBER
    real_den = eigen - wave_sq
    imag_den = wave_sq * DAMPING
    factor = wave_sq / (real_den * real_den + imag_den * imag_den)
    return (factor * real_den, factor * imag_den)


def incident(positions, start_row, row_count):
    heights = jnp.arange(NZ).astype(jnp.float32) + SOURCE_GAP
    across = (start_row + jnp.arange(row_count)).astype(jnp.float32)
    along_y = jnp.arange(NY).astype(jnp.float32)
    source_x = positions[:, 0].astype(jnp.float32)
    source_y = positions[:, 1].astype(jnp.float32)
    offset_x = across[None, :] - source_x[:, None]
    offset_y = along_y[None, :] - source_y[:, None]
    dist_sq = (
        heights[None, :, None, None] * heights[None, :, None, None]
        + offset_x[:, None, :, None] * offset_x[:, None, :, None]
    )
    dist_sq = dist_sq + offset_y[:, None, None, :] * offset_y[:, None, None, :]
    phases = WAVENUMBER * jnp.sqrt(dist_sq)
    return (jnp.cos(phases), jnp.sin(phases))


def dft_table(length, orient, factor):
    indices = jnp.arange(length)
    turn_index = indices[:, None] * indices[None, :] % length
    angles = 2.0 * math.pi / length * turn_index.astype(jnp.float32)
    cosine = jnp.cos(angles) * factor
    sine_part = orient * jnp.sin(angles) * factor
    upper_rows = jnp.stack([cosine, sine_part], axis=1)
    bottom = jnp.stack([-sine_part, cosine], axis=1)
    return jnp.stack([upper_rows, bottom], axis=0)


def apply_table(table, fields, pattern):
    return jnp.einsum(pattern, table, fields, precision=lax.Precision.HIGHEST)


def times_green(spectrum, green_real, green_imag):
    real_part = spectrum[:, 0] * green_real - spectrum[:, 1] * green_imag
    imag_part = spectrum[:, 0] * green_imag + spectrum[:, 1] * green_real
    return jnp.stack([real_part, imag_part], axis=1)


def transform(fields, spectral, tables):
    z_forward, x_forward, y_forward, z_inverse, x_inverse, y_inverse = tables
    depth_done = apply_table(z_forward, fields, DEPTH_PATTERN)
    planes = apply_table(
        x_forward,
        lax.all_to_all(depth_done, "space", split_axis=2, concat_axis=3, tiled=True),
        FIRST_PATTERN,
    )
    spectrum = spectral(apply_table(y_forward, planes, SECOND_PATTERN))
    returned = apply_table(
        x_inverse, apply_table(y_inverse, spectrum, SECOND_PATTERN), FIRST_PATTERN
    )
    return apply_table(
        z_inverse,
        lax.all_to_all(returned, "space", split_axis=3, concat_axis=2, tiled=True),
        DEPTH_PATTERN,
    )


def descent_total(descent):
    local_sum = jnp.sum(descent * descent)
    return lax.psum(local_sum, ("src", "space"))


def bounded(numerator, power_sum, total_sources):
    floored = jnp.maximum(power_sum, FLOOR_SHARE * total_sources)
    return jnp.stack(
        [
            jnp.clip(numerator[0] / floored, REAL_LOW, REAL_HIGH),
            jnp.clip(numerator[1] / floored, 0.0, IMAG_HIGH),
        ],
        axis=0,
    )


def on_device(contrast, measured, positions):
    spaces = lax.axis_size("space")
    sources = positions.shape[0]
    row_count = contrast.shape[2]
    plane_count = NZ // spaces
    start_row = lax.axis_index("space") * row_count
    total_sources = sources * lax.axis_size("src")
    chi_real, chi_imag = (contrast[0], contrast[1])
    inc_real, inc_imag = incident(positions, start_row, row_count)
    tables = (
        dft_table(NZ, 1.0, 1.0),
        dft_table(NX, 1.0, 1.0),
        dft_table(NY, 1.0, 1.0),
        dft_table(NZ, -1.0, 1.0 / NZ),
        dft_table(NX, -1.0, 1.0 / NX),
        dft_table(NY, -1.0, 1.0 / NY),
    )
    green_real, green_imag = green_spectrum(
        laplace_modes(lax.axis_index("space") * plane_count, plane_count, NZ),
        laplace_modes(0, NX, NX),
        laplace_modes(0, NY, NY),
    )
    forward_green = partial(times_green, green_real=green_real, green_imag=green_imag)
    adjoint_green = partial(times_green, green_real=green_real, green_imag=-green_imag)
    sources_field = jnp.stack(
        [chi_real * inc_real - chi_imag * inc_imag, chi_real * inc_imag + chi_imag * inc_real],
        axis=1,
    )
    scattered = transform(sources_field, forward_green, tables)
    data_real = measured[:, 0]
    data_imag = measured[:, 1]
    data_local = jnp.sum(data_real * data_real + data_imag * data_imag)
    for outer_step in range(OUTER):
        chi_inc_real = chi_real * inc_real - chi_imag * inc_imag
        chi_inc_imag = chi_real * inc_imag + chi_imag * inc_real
        object_local = jnp.sum(chi_inc_real * chi_inc_real + chi_inc_imag * chi_inc_imag)
        data_total, object_total = lax.psum((data_local, object_local), ("src", "space"))
        data_weight = 1.0 / data_total
        object_weight = 1.0 / object_total
        total_real = inc_real + scattered[:, 0]
        total_imag = inc_imag + scattered[:, 1]
        resid_real = chi_real * total_real - chi_imag * total_imag - sources_field[:, 0]
        resid_imag = chi_real * total_imag + chi_imag * total_real - sources_field[:, 1]
        adjoint_real = -object_weight * (chi_real * resid_real + chi_imag * resid_imag)
        adjoint_imag = -object_weight * (chi_real * resid_imag - chi_imag * resid_real)
        adjoint_real = adjoint_real.at[:, 0].add(data_weight * (data_real - scattered[:, 0, 0]))
        adjoint_imag = adjoint_imag.at[:, 0].add(data_weight * (data_imag - scattered[:, 1, 0]))
        adjoint_input = jnp.stack([adjoint_real, adjoint_imag], axis=1)
        residual = jnp.stack([resid_real, resid_imag], axis=1)
        adjoint_image = transform(adjoint_input, adjoint_green, tables)
        descent = object_weight * residual + adjoint_image
        descent_early = descent_total(descent)
        descent_image = transform(descent, forward_green, tables)
        image_real = descent_image[:, 0]
        image_imag = descent_image[:, 1]
        change_real = descent[:, 0] - (chi_real * image_real - chi_imag * image_imag)
        change_imag = descent[:, 1] - (chi_real * image_imag + chi_imag * image_real)
        image_local = jnp.sum(
            image_real[:, 0] * image_real[:, 0] + image_imag[:, 0] * image_imag[:, 0]
        )
        change_local = jnp.sum(change_real * change_real + change_imag * change_imag)
        image_total, change_total = lax.psum((image_local, change_local), ("src", "space"))
        step_length = descent_early / (data_weight * image_total + object_weight * change_total)
        sources_field = sources_field + step_length * descent
        scattered = scattered + step_length * descent_image
        total_real = inc_real + scattered[:, 0]
        total_imag = inc_imag + scattered[:, 1]
        numerator_real = jnp.sum(
            sources_field[:, 0] * total_real + sources_field[:, 1] * total_imag, axis=0
        )
        numerator_imag = jnp.sum(
            sources_field[:, 1] * total_real - sources_field[:, 0] * total_imag, axis=0
        )
        power_sum = jnp.sum(total_real * total_real + total_imag * total_imag, axis=0)
        numerator = jnp.stack([numerator_real, numerator_imag], axis=0)
        numerator_all, power_all = lax.psum((numerator, power_sum), "src")
        contrast_now = bounded(numerator_all, power_all, total_sources)
        chi_real = contrast_now[0]
        chi_imag = contrast_now[1]
    return (sources_field, contrast_now)


def solution(mesh):
    placed = (P(None, None, "space", None), P("src", None, "space", None), P("src", None))
    return jax.shard_map(
        on_device,
        mesh=mesh,
        in_specs=placed,
        out_specs=(P("src", None, None, "space", None), P(None, None, "space", None)),
        check_vma=False,
    )
```

profile of v0, /device:TPU:8, one launch (start us, length us, event | category | flops | bytes accessed | tf_op | source)
XLA Modules:
  0.0 783.4 jit_solution(12502016712081461501)
XLA Ops:
  10.4 6.7 copy_cosine_fusion
  22.7 13.0 %all-to-all-start = ((f32[1,2,64,4,256]{4,1,3,0,2:T(2,128)}), f32[1,2,64,4,256]{4,1,3,0,2:T(2,128)}, u32[]{:S(2)}, u32[]{:S(2)}) async-start(f32[1,2,64,4,256]{4,1,3,0,2:T(2,128)} %copy.363), calls=%async_computation | async-start | bytes 1048576 | tf_op jit(solution)/shard_map/all_to_all | solution.py:82
  40.1 12.9 %all-to-all-done = f32[1,2,64,4,256]{4,1,3,0,2:T(2,128)} async-done(((f32[1,2,64,4,256]{4,1,3,0,2:T(2,128)}), f32[1,2,64,4,256]{4,1,3,0,2:T(2,128)}, u32[]{:S(2)}, u32[]{:S(2)}) %all-to-all-start) | async-done | bytes 524320 | tf_op jit(solution)/shard_map/all_to_all | solution.py:82
  64.9 6.1 all-to-all-start.1
  73.0 76.7 %all-reduce.2 = (f32[]{:T(128)}, f32[]{:T(128)}) all-reduce(f32[]{:T(128)} %get-tuple-element.82, f32[]{:T(128)} %get-tuple-element.133), channel_id=1, replica_groups=mesh['src'=4,'space'=64] {'src','space'}, use_global_device_ids=true, to_apply=%region_1.2 | all-reduce | flops 2 | bytes 16 | tf_op jit(solution)/shard_map/psum | solution.py:148
  154.8 7.7 add_multiply_fusion.1
  165.8 26.7 %all_to_all.40 = f32[1,2,64,4,256]{4,1,3,0,2:T(2,128)S(1)} all-to-all(f32[1,2,64,4,256]{4,1,3,0,2:T(2,128)S(1)} %copy.380), channel_id=1, replica_groups=mesh['src'=4,'space'=64] {'space'}, dimensions={2} | all-to-all | bytes 1048576 | tf_op jit(solution)/shard_map/all_to_all | solution.py:82
  199.8 6.2 all-to-all-start.3
  207.8 15.7 %all-to-all-done.3 = f32[1,2,1,256,256]{4,1,2,0,3:T(2,128)} async-done(((f32[1,2,1,256,256]{4,1,2,0,3:T(2,128)}), f32[1,2,1,256,256]{4,1,2,0,3:T(2,128)}, u32[]{:S(2)}, u32[]{:S(2)}) %all-to-all-start.3) | async-done | bytes 524320 | tf_op jit(solution)/shard_map/all_to_all | solution.py:91
  227.5 23.7 %all_to_all.41 = f32[1,2,64,4,256]{4,1,3,0,2:T(2,128)} all-to-all(f32[1,2,64,4,256]{4,1,3,0,2:T(2,128)S(1)} %copy.388), channel_id=1, replica_groups=mesh['src'=4,'space'=64] {'space'}, dimensions={2} | all-to-all | bytes 1048576 | tf_op jit(solution)/shard_map/all_to_all | solution.py:82
  263.2 6.1 all-to-all-start.5
  270.2 16.6 %all-to-all-done.5 = f32[1,2,1,256,256]{4,1,2,0,3:T(2,128)} async-done(((f32[1,2,1,256,256]{4,1,2,0,3:T(2,128)}), f32[1,2,1,256,256]{4,1,2,0,3:T(2,128)}, u32[]{:S(2)}, u32[]{:S(2)}) %all-to-all-start.5) | async-done | bytes 524320 | tf_op jit(solution)/shard_map/all_to_all | solution.py:91
  291.7 73.1 %all-reduce.1 = (f32[]{:T(128)}, f32[]{:T(128)}, f32[]{:T(128)}) all-reduce(f32[]{:T(128)} %get-tuple-element.77, f32[]{:T(128)} %fusion.95, f32[]{:T(128)} %fusion.62), channel_id=1, replica_groups=mesh['src'=4,'space'=64] {'src','space'}, use_global_device_ids=true, to_apply=%region_5.6 | all-reduce | flops 3 | bytes 24 | tf_op jit(solution)/shard_map/psum | solution.py:98
  376.1 45.6 %all-reduce.10.cloned.1.call-done = (f32[2,64,4,256]{3,2,1,0:T(4,128)}, f32[64,4,256]{2,1,0:T(4,128)}) async-done(((f32[2,64,4,256]{3,2,1,0:T(4,128)}, f32[64,4,256]{2,1,0:T(4,128)}), (f32[2,64,4,256]{3,2,1,0:T(4,128)}, f32[64,4,256]{2,1,0:T(4,128)})) %all-reduce.10.cloned.1.call-update) | async-done | bytes 786448 | tf_op jit(solution)/shard_map/psum | solution.py:187
  429.2 74.8 %psum.101 = f32[]{:T(128)} all-reduce(f32[]{:T(128)} %add_reduce_fusion), channel_id=1, replica_groups=mesh['src'=4,'space'=64] {'src','space'}, use_global_device_ids=true, to_apply=%region_13.14 | all-reduce | flops 1 | bytes 8 | tf_op jit(solution)/shard_map/psum | solution.py:148
  512.7 26.4 %all_to_all.42 = f32[1,2,64,4,256]{4,1,3,0,2:T(2,128)} all-to-all(f32[1,2,64,4,256]{4,1,3,0,2:T(2,128)S(1)} %copy.427), channel_id=1, replica_groups=mesh['src'=4,'space'=64] {'space'}, dimensions={2} | all-to-all | bytes 1048576 | tf_op jit(solution)/shard_map/all_to_all | solution.py:82
  547.4 6.2 all-to-all-start.7
  555.6 15.5 %all-to-all-done.7 = f32[1,2,1,256,256]{4,1,2,0,3:T(2,128)} async-done(((f32[1,2,1,256,256]{4,1,2,0,3:T(2,128)}), f32[1,2,1,256,256]{4,1,2,0,3:T(2,128)}, u32[]{:S(2)}, u32[]{:S(2)}) %all-to-all-start.7) | async-done | bytes 524320 | tf_op jit(solution)/shard_map/all_to_all | solution.py:91
  575.9 23.7 %all_to_all.43 = f32[1,2,64,4,256]{4,1,3,0,2:T(2,128)} all-to-all(f32[1,2,64,4,256]{4,1,3,0,2:T(2,128)S(1)} %copy.435), channel_id=1, replica_groups=mesh['src'=4,'space'=64] {'space'}, dimensions={2} | all-to-all | bytes 1048576 | tf_op jit(solution)/shard_map/all_to_all | solution.py:82
  609.8 5.9 all-to-all-start.9
  616.1 17.1 %all-to-all-done.9 = f32[1,2,1,256,256]{4,1,2,0,3:T(2,128)S(1)} async-done(((f32[1,2,1,256,256]{4,1,2,0,3:T(2,128)}), f32[1,2,1,256,256]{4,1,2,0,3:T(2,128)S(1)}, u32[]{:S(2)}, u32[]{:S(2)}) %all-to-all-start.9) | async-done | bytes 524320 | tf_op jit(solution)/shard_map/all_to_all | solution.py:91
  636.9 73.1 %all-reduce = (f32[]{:T(128)}, f32[]{:T(128)}, f32[]{:T(128)}) all-reduce(f32[]{:T(128)} %get-tuple-element.72, f32[]{:T(128)} %fusion.96, f32[]{:T(128)} %fusion.44), channel_id=1, replica_groups=mesh['src'=4,'space'=64] {'src','space'}, use_global_device_ids=true, to_apply=%region_15.16 | all-reduce | flops 3 | bytes 24 | tf_op jit(solution)/shard_map/psum | solution.py:98
  718.8 7.3 multiply_add_fusion.1
  728.3 44.7 %all-reduce.8.cloned.1.call-done = (f32[2,64,4,256]{3,0,2,1:T(2,128)}, f32[64,4,256]{2,0,1:T(8,128)}) async-done(((f32[2,64,4,256]{3,0,2,1:T(2,128)}, f32[64,4,256]{2,0,1:T(8,128)}), (f32[2,64,4,256]{3,0,2,1:T(2,128)}, f32[64,4,256]{2,0,1:T(8,128)})) %all-reduce.8.cloned.1.call-update) | async-done | bytes 786448 | tf_op jit(solution)/shard_map/psum | solution.py:187
  (234 shorter events, 129.1 us)
Async XLA Ops:
  7.2 10.0 %copy-start.44 = (f32[2,64,4,256]{3,2,1,0:T(4,128)S(1)}, f32[2,64,4,256]{3,2,1,0:T(4,128)}, u32[]{:S(2)}) copy-start(f32[2,64,4,256]{3,2,1,0:T(4,128)} %param.11) | copy-start | bytes 1572868
  10.2 6.9 copy-start.33
  10.4 144.0 %copy-start.12 = (f32[1,64,4,256]{3,2,1,0:T(4,128)}, f32[1,64,4,256]{3,2,1,0:T(4,128)S(1)}, u32[]{:S(2)}) copy-start(f32[1,64,4,256]{3,2,1,0:T(4,128)S(1)} %sqrt_multiply_fusion.1) | copy-start | bytes 786436
  17.2 3.5 copy-start.18
  20.7 133.8 %copy-start.5 = (f32[1,64,4,256]{3,2,1,0:T(4,128)}, f32[1,64,4,256]{3,2,1,0:T(4,128)S(1)}, u32[]{:S(2)}) copy-start(f32[1,64,4,256]{3,2,1,0:T(4,128)S(1)} %get-tuple-element.83) | copy-start | bytes 786436
  20.7 133.8 %copy-start.7 = (f32[1,64,4,256]{3,2,1,0:T(4,128)}, f32[1,64,4,256]{3,2,1,0:T(4,128)S(1)}, u32[]{:S(2)}) copy-start(f32[1,64,4,256]{3,2,1,0:T(4,128)S(1)} %get-tuple-element.84) | copy-start | bytes 786436
  20.7 141.9 %copy-start.3 = (f32[1,64,4,256]{3,2,1,0:T(4,128)}, f32[1,64,4,256]{3,2,1,0:T(4,128)S(1)}, u32[]{:S(2)}) copy-start(f32[1,64,4,256]{3,2,1,0:T(4,128)S(1)} %get-tuple-element.118) | copy-start | bytes 786436
  22.7 30.3 %all-to-all-start = ((f32[1,2,64,4,256]{4,1,3,0,2:T(2,128)}), f32[1,2,64,4,256]{4,1,3,0,2:T(2,128)}, u32[]{:S(2)}, u32[]{:S(2)}) async-start(f32[1,2,64,4,256]{4,1,3,0,2:T(2,128)} %copy.363), calls=%async_computation | async-start | bytes 1048576 | tf_op jit(solution)/shard_map/all_to_all | solution.py:82
  64.9 87.1 %all-to-all-start.1 = ((f32[1,2,1,256,256]{4,1,2,0,3:T(2,128)}), f32[1,2,1,256,256]{4,1,2,0,3:T(2,128)}, u32[]{:S(2)}, u32[]{:S(2)}) async-start(f32[1,2,1,256,256]{4,1,2,0,3:T(2,128)} %copy.367), calls=%async_computation.1 | async-start | bytes 1048576 | tf_op jit(solution)/shard_map/all_to_all | solution.py:91
  154.4 9.3 %copy-start.2 = (f32[1,4,256,2,64]{2,0,1,4,3:T(1,128)}, f32[1,4,256,2,64]{2,0,1,4,3:T(1,128)S(1)}, u32[]{:S(2)}) copy-start(f32[1,4,256,2,64]{2,0,1,4,3:T(1,128)S(1)} %copy.761) | copy-start | bytes 1572868
  199.8 6.2 copy-start.25
  199.8 23.7 %all-to-all-start.3 = ((f32[1,2,1,256,256]{4,1,2,0,3:T(2,128)}), f32[1,2,1,256,256]{4,1,2,0,3:T(2,128)}, u32[]{:S(2)}, u32[]{:S(2)}) async-start(f32[1,2,1,256,256]{4,1,2,0,3:T(2,128)} %copy.384), calls=%async_computation.3 | async-start | bytes 1048576 | tf_op jit(solution)/shard_map/all_to_all | solution.py:91
  207.0 16.5 %copy-start.14 = (f32[1,64,2,64]{3,1,2,0:T(8,128)S(1)}, f32[1,64,2,64]{3,1,2,0:T(8,128)}, u32[]{:S(2)}) copy-start(f32[1,64,2,64]{3,1,2,0:T(8,128)} %get-tuple-element.128) | copy-start | bytes 98308
  207.0 16.5 %copy-start.16 = (f32[1,64,2,64]{3,1,2,0:T(8,128)S(1)}, f32[1,64,2,64]{3,1,2,0:T(8,128)}, u32[]{:S(2)}) copy-start(f32[1,64,2,64]{3,1,2,0:T(8,128)} %get-tuple-element.129) | copy-start | bytes 98308
  263.2 23.6 %all-to-all-start.5 = ((f32[1,2,1,256,256]{4,1,2,0,3:T(2,128)}), f32[1,2,1,256,256]{4,1,2,0,3:T(2,128)}, u32[]{:S(2)}, u32[]{:S(2)}) async-start(f32[1,2,1,256,256]{4,1,2,0,3:T(2,128)} %copy.392), calls=%async_computation.5 | async-start | bytes 1048576 | tf_op jit(solution)/shard_map/all_to_all | solution.py:91
  269.3 152.4 %all-reduce.10.cloned.1.call-start = ((), (), s32[]{:S(2)}) async-start(), calls=%async_computation.11 | async-start | bytes 1572864 | tf_op jit(solution)/shard_map/psum | solution.py:187
  369.6 3.2 copy-start.19
  547.4 6.2 copy-start.21
  547.4 23.7 %all-to-all-start.7 = ((f32[1,2,1,256,256]{4,1,2,0,3:T(2,128)}), f32[1,2,1,256,256]{4,1,2,0,3:T(2,128)}, u32[]{:S(2)}, u32[]{:S(2)}) async-start(f32[1,2,1,256,256]{4,1,2,0,3:T(2,128)} %copy.431), calls=%async_computation.7 | async-start | bytes 1048576 | tf_op jit(solution)/shard_map/all_to_all | solution.py:91
  554.6 16.5 %copy-start.15 = (f32[1,64,2,64]{3,1,2,0:T(8,128)S(1)}, f32[1,64,2,64]{3,1,2,0:T(8,128)}, u32[]{:S(2)}) copy-start(f32[1,64,2,64]{3,1,2,0:T(8,128)} %get-tuple-element.128) | copy-start | bytes 98308
  554.6 16.5 %copy-start.17 = (f32[1,64,2,64]{3,1,2,0:T(8,128)S(1)}, f32[1,64,2,64]{3,1,2,0:T(8,128)}, u32[]{:S(2)}) copy-start(f32[1,64,2,64]{3,1,2,0:T(8,128)} %get-tuple-element.129) | copy-start | bytes 98308
  571.1 1.9 copy-start.41
  609.8 23.5 %all-to-all-start.9 = ((f32[1,2,1,256,256]{4,1,2,0,3:T(2,128)}), f32[1,2,1,256,256]{4,1,2,0,3:T(2,128)S(1)}, u32[]{:S(2)}, u32[]{:S(2)}) async-start(f32[1,2,1,256,256]{4,1,2,0,3:T(2,128)} %copy.439), calls=%async_computation.9 | async-start | bytes 1048576 | tf_op jit(solution)/shard_map/all_to_all | solution.py:91
  615.7 157.4 %all-reduce.8.cloned.1.call-start = ((), (), s32[]{:S(2)}) async-start(), calls=%async_computation.10 | async-start | bytes 1572864 | tf_op jit(solution)/shard_map/psum | solution.py:187
  (33 other events, 33.4 us)
Sparse Core Ops, SparseCore 0:
  376.2 45.4 all-reduce.9
  727.5 45.4 all-reduce.7
where the time goes:
time: 790 us; the launch traced here: 783 us
  blocking collectives  398 us (50%)
  waiting for transfers between devices  168 us (21%)
  other arithmetic  58.6 us (7%)
  local copies, waits for them, and re-layouts  46.7 us (6%)
  matrix products  45.3 us (6%)
  starting transfers between devices  43.6 us (6%)
  between operations  22.5 us (3%)
    psum x2, blocking collectives, on_device(): lax.psum((data_local, object_local), ('src', 'space'))  152 us
    psum x2, blocking collectives, descent_total(): return lax.psum(local_sum, ('src', 'space'))  146 us
    all_to_all x4, blocking collectives, transform(): lax.all_to_all(depth_done, 'space', split_axis=2, concat_axis=3, tiled=True)  101 us
    psum x2, waiting for transfers between devices, on_device(): numerator_all, power_all = lax.psum((numerator, power_sum), 'src')  90.3 us
    all_to_all x5, waiting for transfers between devices, transform(): lax.all_to_all(returned, 'space', split_axis=3, concat_axis=2, tiled=True)  65 us
    dot_general x30, matrix products, apply_table(): return jnp.einsum(pattern, table, fields, precision=lax.Precision.HIGHEST)  45.3 us
    all_to_all x5, starting transfers between devices, transform(): lax.all_to_all(returned, 'space', split_axis=3, concat_axis=2, tiled=True)  30.5 us
  transfers between devices with their start and end apart: 8, of which 7 were waited for; matrix products, arithmetic and copies ran while one was open for 2% of the time, Pallas kernels for 0%

commit v1 on v0

--- a/solution.py
+++ b/solution.py
@@ -145,7 +145,9 @@
         chi_inc_real = chi_real * inc_real - chi_imag * inc_imag
         chi_inc_imag = chi_real * inc_imag + chi_imag * inc_real
         object_local = jnp.sum(chi_inc_real * chi_inc_real + chi_inc_imag * chi_inc_imag)
-        data_total, object_total = lax.psum((data_local, object_local), ("src", "space"))
+        data_total, object_total = jax.lax.psum(
+            jax.lax.psum((data_local, object_local), axis_name="space"), axis_name="src"
+        )
         data_weight = 1.0 / data_total
         object_weight = 1.0 / object_total
         total_real = inc_real + scattered[:, 0]

time: 790 us -> 916 us (1.16)
  blocking collectives: 398 us -> 523 us
    psum x2 -> x4, blocking collectives: 152 us -> 270 us  [the longest x2 248 us: on_device(): jax.lax.psum((data_local, object_local), axis_name='space')]
  transfers between devices with their start and end apart: 8 -> 8, of which waited for: 7 -> 7; matrix products, arithmetic and copies ran while one was open for 2% -> 1% of each run, Pallas kernels for 0% -> 0%
where the time goes in v1:
time: 916 us; the launch traced here: 909 us
  blocking collectives  523 us (57%)
  waiting for transfers between devices  168 us (18%)
  other arithmetic  60.3 us (7%)
  local copies, waits for them, and re-layouts  46 us (5%)
  matrix products  45.4 us (5%)
  starting transfers between devices  43.5 us (5%)
  between operations  22.5 us (2%)
    psum x2, blocking collectives, on_device(): jax.lax.psum((data_local, object_local), axis_name='space')  248 us
    psum x2, blocking collectives, descent_total(): return lax.psum(local_sum, ('src', 'space'))  147 us
    all_to_all x4, blocking collectives, transform(): lax.all_to_all(depth_done, 'space', split_axis=2, concat_axis=3, tiled=True)  107 us
    psum x2, waiting for transfers between devices, on_device(): numerator_all, power_all = lax.psum((numerator, power_sum), 'src')  90.3 us
    all_to_all x5, waiting for transfers between devices, transform(): lax.all_to_all(returned, 'space', split_axis=3, concat_axis=2, tiled=True)  65 us
    dot_general x30, matrix products, apply_table(): return jnp.einsum(pattern, table, fields, precision=lax.Precision.HIGHEST)  45.4 us
    all_to_all x5, starting transfers between devices, transform(): lax.all_to_all(returned, 'space', split_axis=3, concat_axis=2, tiled=True)  30.5 us
    psum x2, blocking collectives, on_device(): jax.lax.psum(jax.lax.psum((data_local, object_local), axis_name='space'),...  21.8 us
  transfers between devices with their start and end apart: 8, of which 7 were waited for; matrix products, arithmetic and copies ran while one was open for 1% of the time, Pallas kernels for 0%

profile of v1, /device:TPU:8, one launch (start us, length us, event | category | flops | bytes accessed | tf_op | source)
XLA Modules:
  0.0 909.3 jit_solution(5066509298838068777)
XLA Ops:
  10.4 6.7 copy_cosine_fusion
  22.6 13.0 %all-to-all-start = ((f32[1,2,64,4,256]{4,1,3,0,2:T(2,128)}), f32[1,2,64,4,256]{4,1,3,0,2:T(2,128)}, u32[]{:S(2)}, u32[]{:S(2)}) async-start(f32[1,2,64,4,256]{4,1,3,0,2:T(2,128)} %copy.363), calls=%async_computation | async-start | bytes 1048576 | tf_op jit(solution)/shard_map/all_to_all | solution.py:82
  40.0 12.9 %all-to-all-done = f32[1,2,64,4,256]{4,1,3,0,2:T(2,128)} async-done(((f32[1,2,64,4,256]{4,1,3,0,2:T(2,128)}), f32[1,2,64,4,256]{4,1,3,0,2:T(2,128)}, u32[]{:S(2)}, u32[]{:S(2)}) %all-to-all-start) | async-done | bytes 524320 | tf_op jit(solution)/shard_map/all_to_all | solution.py:82
  72.9 125.4 %all-reduce.2 = (f32[]{:T(128)}, f32[]{:T(128)}) all-reduce(f32[]{:T(128)} %get-tuple-element.84, f32[]{:T(128)} %get-tuple-element.135), channel_id=1, replica_groups=mesh['src'=4,'space'=64] {'space'}, use_global_device_ids=true, to_apply=%region_1.2 | all-reduce | flops 2 | bytes 16 | tf_op jit(solution)/shard_map/psum | solution.py:149
  198.4 11.3 %all-reduce.3 = (f32[]{:T(128)}, f32[]{:T(128)}) all-reduce(f32[]{:T(128)} %get-tuple-element.66, f32[]{:T(128)} %get-tuple-element.67), channel_id=1, replica_groups=mesh['src'=4,'space'=64] {'src'}, use_global_device_ids=true, to_apply=%region_2.3 | all-reduce | flops 2 | bytes 16 | tf_op jit(solution)/shard_map/psum | solution.py:148
  214.7 7.7 add_multiply_fusion.1
  225.7 31.7 %all_to_all.40 = f32[1,2,64,4,256]{4,1,3,0,2:T(2,128)S(1)} all-to-all(f32[1,2,64,4,256]{4,1,3,0,2:T(2,128)S(1)} %copy.380), channel_id=1, replica_groups=mesh['src'=4,'space'=64] {'space'}, dimensions={2} | all-to-all | bytes 1048576 | tf_op jit(solution)/shard_map/all_to_all | solution.py:82
  264.7 6.2 all-to-all-start.3
  272.6 15.7 %all-to-all-done.3 = f32[1,2,1,256,256]{4,1,2,0,3:T(2,128)} async-done(((f32[1,2,1,256,256]{4,1,2,0,3:T(2,128)}), f32[1,2,1,256,256]{4,1,2,0,3:T(2,128)}, u32[]{:S(2)}, u32[]{:S(2)}) %all-to-all-start.3) | async-done | bytes 524320 | tf_op jit(solution)/shard_map/all_to_all | solution.py:91
  292.4 23.5 %all_to_all.41 = f32[1,2,64,4,256]{4,1,3,0,2:T(2,128)} all-to-all(f32[1,2,64,4,256]{4,1,3,0,2:T(2,128)S(1)} %copy.388), channel_id=1, replica_groups=mesh['src'=4,'space'=64] {'space'}, dimensions={2} | all-to-all | bytes 1048576 | tf_op jit(solution)/shard_map/all_to_all | solution.py:82
  327.9 6.1 all-to-all-start.5
  334.9 16.6 %all-to-all-done.5 = f32[1,2,1,256,256]{4,1,2,0,3:T(2,128)} async-done(((f32[1,2,1,256,256]{4,1,2,0,3:T(2,128)}), f32[1,2,1,256,256]{4,1,2,0,3:T(2,128)}, u32[]{:S(2)}, u32[]{:S(2)}) %all-to-all-start.5) | async-done | bytes 524320 | tf_op jit(solution)/shard_map/all_to_all | solution.py:91
  356.4 73.4 %all-reduce.1 = (f32[]{:T(128)}, f32[]{:T(128)}, f32[]{:T(128)}) all-reduce(f32[]{:T(128)} %get-tuple-element.79, f32[]{:T(128)} %fusion.95, f32[]{:T(128)} %fusion.62), channel_id=1, replica_groups=mesh['src'=4,'space'=64] {'src','space'}, use_global_device_ids=true, to_apply=%region_7.8 | all-reduce | flops 3 | bytes 24 | tf_op jit(solution)/shard_map/psum | solution.py:98
  441.0 45.6 %all-reduce.11.cloned.1.call-done = (f32[2,64,4,256]{3,2,1,0:T(4,128)}, f32[64,4,256]{2,1,0:T(4,128)}) async-done(((f32[2,64,4,256]{3,2,1,0:T(4,128)}, f32[64,4,256]{2,1,0:T(4,128)}), (f32[2,64,4,256]{3,2,1,0:T(4,128)}, f32[64,4,256]{2,1,0:T(4,128)})) %all-reduce.11.cloned.1.call-update) | async-done | bytes 786448 | tf_op jit(solution)/shard_map/psum | solution.py:189
  493.8 122.8 %psum.127 = f32[]{:T(128)} all-reduce(f32[]{:T(128)} %add_reduce_fusion), channel_id=1, replica_groups=mesh['src'=4,'space'=64] {'space'}, use_global_device_ids=true, to_apply=%region_15.16 | all-reduce | flops 1 | bytes 8 | tf_op jit(solution)/shard_map/psum | solution.py:149
  617.9 10.5 %psum.128 = f32[]{:T(128)} all-reduce(f32[]{:T(128)} %psum.127), channel_id=1, replica_groups=mesh['src'=4,'space'=64] {'src'}, use_global_device_ids=true, to_apply=%region_16.17 | all-reduce | flops 1 | bytes 8 | tf_op jit(solution)/shard_map/psum | solution.py:148
  637.3 27.9 %all_to_all.42 = f32[1,2,64,4,256]{4,1,3,0,2:T(2,128)} all-to-all(f32[1,2,64,4,256]{4,1,3,0,2:T(2,128)S(1)} %copy.427), channel_id=1, replica_groups=mesh['src'=4,'space'=64] {'space'}, dimensions={2} | all-to-all | bytes 1048576 | tf_op jit(solution)/shard_map/all_to_all | solution.py:82
  673.5 6.2 all-to-all-start.7
  681.7 15.5 %all-to-all-done.7 = f32[1,2,1,256,256]{4,1,2,0,3:T(2,128)} async-done(((f32[1,2,1,256,256]{4,1,2,0,3:T(2,128)}), f32[1,2,1,256,256]{4,1,2,0,3:T(2,128)}, u32[]{:S(2)}, u32[]{:S(2)}) %all-to-all-start.7) | async-done | bytes 524320 | tf_op jit(solution)/shard_map/all_to_all | solution.py:91
  702.0 23.5 %all_to_all.43 = f32[1,2,64,4,256]{4,1,3,0,2:T(2,128)} all-to-all(f32[1,2,64,4,256]{4,1,3,0,2:T(2,128)S(1)} %copy.435), channel_id=1, replica_groups=mesh['src'=4,'space'=64] {'space'}, dimensions={2} | all-to-all | bytes 1048576 | tf_op jit(solution)/shard_map/all_to_all | solution.py:82
  742.0 17.1 %all-to-all-done.9 = f32[1,2,1,256,256]{4,1,2,0,3:T(2,128)S(1)} async-done(((f32[1,2,1,256,256]{4,1,2,0,3:T(2,128)}), f32[1,2,1,256,256]{4,1,2,0,3:T(2,128)S(1)}, u32[]{:S(2)}, u32[]{:S(2)}) %all-to-all-start.9) | async-done | bytes 524320 | tf_op jit(solution)/shard_map/all_to_all | solution.py:91
  762.7 73.2 %all-reduce = (f32[]{:T(128)}, f32[]{:T(128)}, f32[]{:T(128)}) all-reduce(f32[]{:T(128)} %get-tuple-element.74, f32[]{:T(128)} %fusion.96, f32[]{:T(128)} %fusion.44), channel_id=1, replica_groups=mesh['src'=4,'space'=64] {'src','space'}, use_global_device_ids=true, to_apply=%region_18.19 | all-reduce | flops 3 | bytes 24 | tf_op jit(solution)/shard_map/psum | solution.py:98
  844.6 7.3 multiply_add_fusion.1
  854.2 44.7 %all-reduce.9.cloned.1.call-done = (f32[2,64,4,256]{3,0,2,1:T(2,128)}, f32[64,4,256]{2,0,1:T(8,128)}) async-done(((f32[2,64,4,256]{3,0,2,1:T(2,128)}, f32[64,4,256]{2,0,1:T(8,128)}), (f32[2,64,4,256]{3,0,2,1:T(2,128)}, f32[64,4,256]{2,0,1:T(8,128)})) %all-reduce.9.cloned.1.call-update) | async-done | bytes 786448 | tf_op jit(solution)/shard_map/psum | solution.py:189
  (234 shorter events, 142.0 us)
Async XLA Ops:
  7.2 10.0 %copy-start.43 = (f32[2,64,4,256]{3,2,1,0:T(4,128)S(1)}, f32[2,64,4,256]{3,2,1,0:T(4,128)}, u32[]{:S(2)}) copy-start(f32[2,64,4,256]{3,2,1,0:T(4,128)} %param.11) | copy-start | bytes 1572868
  10.2 6.9 copy-start.32
  10.4 203.9 %copy-start.12 = (f32[1,64,4,256]{3,2,1,0:T(4,128)}, f32[1,64,4,256]{3,2,1,0:T(4,128)S(1)}, u32[]{:S(2)}) copy-start(f32[1,64,4,256]{3,2,1,0:T(4,128)S(1)} %sqrt_multiply_fusion.1) | copy-start | bytes 786436
  17.2 3.5 copy-start.18
  20.6 193.7 %copy-start.5 = (f32[1,64,4,256]{3,2,1,0:T(4,128)}, f32[1,64,4,256]{3,2,1,0:T(4,128)S(1)}, u32[]{:S(2)}) copy-start(f32[1,64,4,256]{3,2,1,0:T(4,128)S(1)} %get-tuple-element.85) | copy-start | bytes 786436
  20.6 193.7 %copy-start.7 = (f32[1,64,4,256]{3,2,1,0:T(4,128)}, f32[1,64,4,256]{3,2,1,0:T(4,128)S(1)}, u32[]{:S(2)}) copy-start(f32[1,64,4,256]{3,2,1,0:T(4,128)S(1)} %get-tuple-element.86) | copy-start | bytes 786436
  20.6 201.9 %copy-start.3 = (f32[1,64,4,256]{3,2,1,0:T(4,128)}, f32[1,64,4,256]{3,2,1,0:T(4,128)S(1)}, u32[]{:S(2)}) copy-start(f32[1,64,4,256]{3,2,1,0:T(4,128)S(1)} %get-tuple-element.120) | copy-start | bytes 786436
  22.6 30.3 %all-to-all-start = ((f32[1,2,64,4,256]{4,1,3,0,2:T(2,128)}), f32[1,2,64,4,256]{4,1,3,0,2:T(2,128)}, u32[]{:S(2)}, u32[]{:S(2)}) async-start(f32[1,2,64,4,256]{4,1,3,0,2:T(2,128)} %copy.363), calls=%async_computation | async-start | bytes 1048576 | tf_op jit(solution)/shard_map/all_to_all | solution.py:82
  64.9 147.0 %all-to-all-start.1 = ((f32[1,2,1,256,256]{4,1,2,0,3:T(2,128)}), f32[1,2,1,256,256]{4,1,2,0,3:T(2,128)}, u32[]{:S(2)}, u32[]{:S(2)}) async-start(f32[1,2,1,256,256]{4,1,2,0,3:T(2,128)} %copy.367), calls=%async_computation.1 | async-start | bytes 1048576 | tf_op jit(solution)/shard_map/all_to_all | solution.py:91
  214.3 9.3 %copy-start.2 = (f32[1,4,256,2,64]{2,0,1,4,3:T(1,128)}, f32[1,4,256,2,64]{2,0,1,4,3:T(1,128)S(1)}, u32[]{:S(2)}) copy-start(f32[1,4,256,2,64]{2,0,1,4,3:T(1,128)S(1)} %copy.761) | copy-start | bytes 1572868
  264.7 6.2 copy-start.25
  264.7 23.7 %all-to-all-start.3 = ((f32[1,2,1,256,256]{4,1,2,0,3:T(2,128)}), f32[1,2,1,256,256]{4,1,2,0,3:T(2,128)}, u32[]{:S(2)}, u32[]{:S(2)}) async-start(f32[1,2,1,256,256]{4,1,2,0,3:T(2,128)} %copy.384), calls=%async_computation.3 | async-start | bytes 1048576 | tf_op jit(solution)/shard_map/all_to_all | solution.py:91
  271.9 16.5 %copy-start.14 = (f32[1,64,2,64]{3,1,2,0:T(8,128)S(1)}, f32[1,64,2,64]{3,1,2,0:T(8,128)}, u32[]{:S(2)}) copy-start(f32[1,64,2,64]{3,1,2,0:T(8,128)} %get-tuple-element.130) | copy-start | bytes 98308
  271.9 16.5 %copy-start.16 = (f32[1,64,2,64]{3,1,2,0:T(8,128)S(1)}, f32[1,64,2,64]{3,1,2,0:T(8,128)}, u32[]{:S(2)}) copy-start(f32[1,64,2,64]{3,1,2,0:T(8,128)} %get-tuple-element.131) | copy-start | bytes 98308
  288.4 1.9 copy-start.39
  327.9 23.6 %all-to-all-start.5 = ((f32[1,2,1,256,256]{4,1,2,0,3:T(2,128)}), f32[1,2,1,256,256]{4,1,2,0,3:T(2,128)}, u32[]{:S(2)}, u32[]{:S(2)}) async-start(f32[1,2,1,256,256]{4,1,2,0,3:T(2,128)} %copy.392), calls=%async_computation.5 | async-start | bytes 1048576 | tf_op jit(solution)/shard_map/all_to_all | solution.py:91
  334.0 152.6 %all-reduce.11.cloned.1.call-start = ((), (), s32[]{:S(2)}) async-start(), calls=%async_computation.11 | async-start | bytes 1572864 | tf_op jit(solution)/shard_map/psum | solution.py:189
  434.6 3.2 copy-start.19
  673.5 6.2 copy-start.21
  673.5 23.7 %all-to-all-start.7 = ((f32[1,2,1,256,256]{4,1,2,0,3:T(2,128)}), f32[1,2,1,256,256]{4,1,2,0,3:T(2,128)}, u32[]{:S(2)}, u32[]{:S(2)}) async-start(f32[1,2,1,256,256]{4,1,2,0,3:T(2,128)} %copy.431), calls=%async_computation.7 | async-start | bytes 1048576 | tf_op jit(solution)/shard_map/all_to_all | solution.py:91
  680.7 16.5 %copy-start.15 = (f32[1,64,2,64]{3,1,2,0:T(8,128)S(1)}, f32[1,64,2,64]{3,1,2,0:T(8,128)}, u32[]{:S(2)}) copy-start(f32[1,64,2,64]{3,1,2,0:T(8,128)} %get-tuple-element.130) | copy-start | bytes 98308
  680.7 16.5 %copy-start.17 = (f32[1,64,2,64]{3,1,2,0:T(8,128)S(1)}, f32[1,64,2,64]{3,1,2,0:T(8,128)}, u32[]{:S(2)}) copy-start(f32[1,64,2,64]{3,1,2,0:T(8,128)} %get-tuple-element.131) | copy-start | bytes 98308
  735.7 23.4 %all-to-all-start.9 = ((f32[1,2,1,256,256]{4,1,2,0,3:T(2,128)}), f32[1,2,1,256,256]{4,1,2,0,3:T(2,128)S(1)}, u32[]{:S(2)}, u32[]{:S(2)}) async-start(f32[1,2,1,256,256]{4,1,2,0,3:T(2,128)} %copy.439), calls=%async_computation.9 | async-start | bytes 1048576 | tf_op jit(solution)/shard_map/all_to_all | solution.py:91
  741.6 157.3 %all-reduce.9.cloned.1.call-start = ((), (), s32[]{:S(2)}) async-start(), calls=%async_computation.10 | async-start | bytes 1572864 | tf_op jit(solution)/shard_map/psum | solution.py:189
  (32 other events, 32.7 us)
Sparse Core Ops, SparseCore 0:
  441.1 45.4 all-reduce.10
  853.4 45.4 all-reduce.8
